TPU v7x, 32 devices: a whole 2x2x4 slice. The times are simulated.
32 devices in a mesh: groups: 2 (over x), row: 4 (over y, core), col: 4 (over z).
Axes of the slice: x: 2, y: 2, z: 4, core: 2. Of those that a mesh axis runs over, the one named last changes fastest.
Arguments:
- observed: float32 [2048, 2048], P(('groups', 'row'), 'col'), parts along dimension 0, may hold values from -24 to 24
- estimate: float32 [2048, 2048], P(('groups', 'row'), 'col'), parts along dimension 0, may hold values from -6 to 6
- kernel: float32 [512, 256], P(('groups', 'row')), parts along dimension 0, may hold values from -6 to 6
Outputs:
- refined: float32 [2048, 2048], P(('groups', 'row'), 'col'), parts along dimension 0
- new_kernel: float32 [512, 256], P(('groups', 'row')), parts along dimension 0
There are 2 independent parts, one for each index of `groups`. A program takes and returns all parts, laid end to end along the dimension named above; each array names one. Nothing has to cross between parts.
All inputs are finite; a program needn't handle non-finite values.
Results may differ from a plain program's by a relative error of at most 0.0001.
Values sent between devices are 32-bit elements; how exact they have to be, the bound alone decides.
A program may use at most 128 MiB of HBM per device.

v0:
```python
import math
import jax
import jax.numpy as jnp
from jax import lax
from jax.sharding import PartitionSpec as P

HIGHEST = lax.Precision.HIGHEST
EPSILON = 1e-06


def padded(block, sides, width):
    for axis, dim in sides:
        count = lax.axis_size(axis)
        forward = [(i, i + 1) for i in range(count - 1)]
        backward = [(target, source) for source, target in forward]
        low = lax.ppermute(
            lax.slice_in_dim(block, block.shape[dim] - width, None, axis=dim), axis, forward
        )
        high = lax.ppermute(lax.slice_in_dim(block, 0, width, axis=dim), axis, backward)
        block = jnp.concatenate([low, block, high], axis=dim)
    return block


def tables(places, length):
    freqs = jnp.arange(length, dtype=jnp.int32)
    phase = jnp.mod(places[:, None] * freqs[None, :], length).astype(jnp.float32) * (
        2.0 * math.pi / length
    )
    return (jnp.cos(phase), jnp.sin(phase))


def forward(field, row_tables, col_tables):
    rows_long = row_tables[0].shape[1]
    cols_long = col_tables[0].shape[1]
    across = jnp.dot(field, jnp.concatenate(col_tables, 1), precision=HIGHEST)
    stacked = lax.dot_general(
        jnp.concatenate(row_tables, 1), across, (((0,), (0,)), ((), ())), precision=HIGHEST
    )
    real_part = stacked[:rows_long, :cols_long] - stacked[rows_long:, cols_long:]
    imag_part = -(stacked[rows_long:, :cols_long] + stacked[:rows_long, cols_long:])
    return (real_part, imag_part)


def inverse(real_part, imag_part, row_tables, col_tables):
    rows_long, cols_long = real_part.shape
    out_rows = row_tables[0].shape[0]
    stacked = jnp.dot(
        jnp.concatenate(row_tables, 0),
        jnp.concatenate([real_part, imag_part], 1),
        precision=HIGHEST,
    )
    mixed_re = stacked[:out_rows, :cols_long] - stacked[out_rows:, cols_long:]
    mixed_im = stacked[out_rows:, :cols_long] + stacked[:out_rows, cols_long:]
    result = lax.dot_general(
        jnp.concatenate([mixed_re, mixed_im], 1),
        jnp.concatenate([col_tables[0], -col_tables[1]], 1),
        (((1,), (1,)), ((), ())),
        precision=HIGHEST,
    )
    return result / (rows_long * cols_long)


def collect(kernel):
    return lax.all_gather(kernel, "row", axis=0, tiled=True)


def per_device(observed, estimate, kernel):
    tile_rows, tile_cols = observed.shape
    owner_rows, kernel_side = kernel.shape
    margin = kernel_side // 2
    rows_long = tile_rows + kernel_side
    cols_long = tile_cols + kernel_side
    factor = 1.0 / kernel_side
    ext_rows = tables(jnp.arange(rows_long, dtype=jnp.int32), rows_long)
    ext_cols = tables(jnp.arange(cols_long, dtype=jnp.int32), cols_long)
    own_rows = tables(jnp.arange(tile_rows, dtype=jnp.int32) + margin, rows_long)
    own_cols = tables(jnp.arange(tile_cols, dtype=jnp.int32) + margin, cols_long)
    lag_rows = tables(jnp.arange(kernel_side, dtype=jnp.int32) - margin, rows_long)
    lag_cols = tables(jnp.arange(kernel_side, dtype=jnp.int32) - margin, cols_long)
    image = estimate
    owned = kernel
    full_kernel = collect(kernel)
    widened = padded(image, (("row", 0), ("col", 1)), margin)
    image_re, image_im = forward(widened, ext_rows, ext_cols)
    kernel_re, kernel_im = forward(full_kernel, lag_rows, lag_cols)
    predicted = (
        inverse(
            image_re * kernel_re - image_im * kernel_im,
            image_re * kernel_im + image_im * kernel_re,
            own_rows,
            own_cols,
        )
        * factor
    )
    residual = predicted - observed
    local_squares = jnp.sum(residual * residual)
    loss = 0.5 * lax.psum(local_squares, ("row", "col"))
    wide_residual = padded(residual, (("row", 0), ("col", 1)), margin)
    resid_re, resid_im = forward(wide_residual, ext_rows, ext_cols)
    image_grad = (
        inverse(
            resid_re * kernel_re + resid_im * kernel_im,
            resid_im * kernel_re - resid_re * kernel_im,
            own_rows,
            own_cols,
        )
        * factor
    )
    tile_re, tile_im = forward(residual, own_rows, own_cols)
    kernel_grad = (
        inverse(
            tile_re * image_re + tile_im * image_im,
            tile_im * image_re - tile_re * image_im,
            lag_rows,
            lag_cols,
        )
        * factor
    )
    grad_squares = jnp.sum(image_grad * image_grad)
    image_norm = lax.psum(grad_squares, ("row", "col"))
    owner_grad = lax.psum_scatter(kernel_grad, "row", scatter_dimension=0, tiled=True)
    owner_grad = lax.psum(owner_grad, "col")
    kernel_norm = lax.psum(jnp.sum(owner_grad * owner_grad), "row")
    owned = owned - 0.25 * loss / (kernel_norm + EPSILON) * owner_grad
    image = image - loss / (image_norm + EPSILON) * image_grad
    return (image, owned)


def solution(mesh):
    placed = (P(("groups", "row"), "col"), P(("groups", "row"), "col"), P(("groups", "row"), None))
    return jax.shard_map(
        per_device,
        mesh=mesh,
        in_specs=placed,
        out_specs=(P(("groups", "row"), "col"), P(("groups", "row"), None)),
        check_vma=False,
    )
```

profile of v0, /device:TPU:0, one launch (start us, length us, event | category | flops | bytes accessed | tf_op | source)
XLA Modules:
  0.0 264.5 jit_solution(6838239969392656546)
XLA Ops:
  7.2 0.0 reduce-scatter.2.cloned.1.call-start
  7.2 1.1 fusion.130
  8.3 2.4 collective-permute-start
  10.7 1.3 collective-permute-start.1
  12.0 0.0 copy-start.28
  12.0 4.3 %fusion.109 = (f32[256,768]{1,0:T(8,128)}, f32[256,768]{1,0:T(8,128)S(1)}, f32[256,768]{1,0:T(8,128)S(1)}) fusion(s32[256]{0:T(256)S(1)} %iota_add_fusion.1), kind=kLoop, calls=%fused_computation.148 | loop fusion | flops 1966080 | bytes 2360320 | tf_op jit(solution)/shard_map/neg | solution.py:56
  16.2 2.1 fusion.111
  18.4 9.1 %all_gather.3 = f32[256,256]{1,0:T(8,128)S(1)} all-gather(f32[64,256]{1,0:T(8,128)S(1)} %copy-done.28), channel_id=1, replica_groups=mesh['groups'=2,'row'=4,'col'=4] {'row'}, dimensions={0}, use_global_device_ids=true | all-gather | bytes 327680 | tf_op jit(solution)/shard_map/all_gather | solution.py:64
  27.5 8.3 %fusion.58 = (f32[512,768]{1,0:T(8,128)}, f32[512,768]{1,0:T(8,128)}, f32[512,768]{1,0:T(8,128)S(1)}) fusion(s32[512]{0:T(512)S(1)} %iota_add_fusion), kind=kLoop, calls=%fused_computation.80 | loop fusion | flops 3932160 | bytes 4720640 | tf_op jit(solution)/shard_map/sin | solution.py:29
  35.9 2.7 %fusion.27 = f32[1536,256]{1,0:T(8,128)S(1)} fusion(f32[256,256]{1,0:T(8,128)S(1)} %all_gather.3, f32[256,768]{1,0:T(8,128)S(1)} %get-tuple-element.32, f32[256,768]{1,0:T(8,128)S(1)} %get-tuple-element.31), kind=kOutput, calls=%fused_computation.36 | convolution fusion | flops 1208352768 | bytes 3407872 | tf_op jit(solution)/shard_map/dot_general | solution.py:35
  38.6 11.0 %fusion.64 = f32[1024,1536]{1,0:T(8,128)S(1)} fusion(f32[1536,256]{1,0:T(8,128)S(1)} %fusion.27, f32[256,512]{1,0:T(8,128)S(1)} %get-tuple-element.36, f32[256,512]{1,0:T(8,128)S(1)} %get-tuple-element.35), kind=kOutput, calls=%fused_computation.93 | convolution fusion | flops 4832100352 | bytes 8912896 | tf_op jit(solution)/shard_map/dot_general | solution.py:36
  49.6 9.5 %fusion.22 = (f32[768,768]{1,0:T(8,128)S(1)}, f32[768,768]{1,0:T(8,128)S(1)}) fusion(), kind=kLoop, calls=%fused_computation.28 | loop fusion | flops 5308416 | bytes 4718592 | tf_op jit(solution)/shard_map/sin | solution.py:29
  59.1 0.0 copy-start.18
  59.1 4.5 %fusion.103 = (f32[512,512]{1,0:T(8,128)S(1)}, f32[512,512]{1,0:T(8,128)S(1)}) fusion(), kind=kLoop, calls=%fused_computation.142 | loop fusion | flops 3670016 | bytes 2097152 | tf_op jit(solution)/shard_map/sin | solution.py:29
  63.6 0.0 collective-permute-done
  63.8 3.5 %collective-permute-start.2 = (f32[512,128]{1,0:T(8,128)S(1)}, f32[512,128]{1,0:T(8,128)S(1)}, u32[]{:S(2)}, u32[]{:S(2)}) collective-permute-start(f32[512,128]{1,0:T(8,128)S(1)} %get-tuple-element.21), channel_id=1, source_target_pairs={{0,1},{1,2},{2,3},{4,5},{5,6},{6,7},{8,9},{9,10},{10,11},{12,13},{... | collective-permute-start | bytes 786440 | tf_op jit(solution)/shard_map/ppermute | solution.py:16
  67.3 1.3 collective-permute-start.3
  68.6 3.2 %fusion.113 = (f32[256,512]{1,0:T(8,128)}, f32[256,512]{1,0:T(8,128)}) fusion(s32[256]{0:T(256)S(1)} %iota_add_fusion.2), kind=kLoop, calls=%fused_computation.155 | loop fusion | flops 1835008 | bytes 1049600 | tf_op jit(solution)/shard_map/cos | solution.py:29
  71.8 1.5 collective-permute-done.2
  73.3 4.1 %collective-permute-done.3 = f32[512,128]{1,0:T(8,128)S(1)} collective-permute-done((f32[512,128]{1,0:T(8,128)S(1)}, f32[512,128]{1,0:T(8,128)S(1)}, u32[]{:S(2)}, u32[]{:S(2)}) %collective-permute-start.3) | collective-permute-done | bytes 262176 | tf_op jit(solution)/shard_map/ppermute | solution.py:19
  77.5 7.7 %fusion.1 = f32[512,1536]{1,0:T(8,128)S(1)} fusion(f32[768,768]{1,0:T(8,128)S(1)} %get-tuple-element.41, f32[768,768]{1,0:T(8,128)S(1)} %get-tuple-element.42, f32[512,128]{1,0:T(8,128)S(1)} %collective-permute-done.3, f32[512,512]{1,0:T(8,128)S(1)} %constant_dynamic-update-slice_fusion, f32[512,128]{1,0:T(8,128)S(1)} %collective-permute-done.2), kind=kOutput, calls=%fused_computation.2 | convolution fusion | flops 7249723392 | bytes 9437184 | tf_op jit(solution)/shard_map/dot_general | solution.py:35
  85.2 11.2 %fusion.26 = f32[1024,1536]{1,0:T(8,128)S(1)} fusion(f32[512,1536]{1,0:T(8,128)S(1)} %fusion.1, f32[512,512]{1,0:T(8,128)S(1)} %get-tuple-element.43, f32[512,512]{1,0:T(8,128)S(1)} %get-tuple-element.44), kind=kOutput, calls=%fused_computation.35 | convolution fusion | flops 9664200704 | bytes 11534336 | tf_op jit(solution)/shard_map/dot_general | solution.py:36
  96.4 3.1 %multiply_subtract_fusion.2 = (f32[512,768]{1,0:T(8,128)}, f32[512,768]{1,0:T(8,128)}, f32[512,768]{1,0:T(8,128)}, f32[512,768]{1,0:T(8,128)S(1)}, f32[512,768]{1,0:T(8,128)}) fusion(f32[1024,1536]{1,0:T(8,128)S(1)} %fusion.26, f32[1024,1536]{1,0:T(8,128)S(1)} %fusion.64), kind=kLoop, calls=%fused_computation.83 | loop fusion | flops 2752512 | bytes 20447232 | tf_op jit(solution)/shard_map/sub | solution.py:88
  99.5 2.9 %multiply_add_fusion.2 = f32[512,768]{1,0:T(8,128)S(1)} fusion(f32[512,768]{1,0:T(8,128)} %get-tuple-element.8, f32[512,768]{1,0:T(8,128)} %get-tuple-element.6, f32[512,768]{1,0:T(8,128)} %get-tuple-element.5, f32[512,768]{1,0:T(8,128)S(1)} %get-tuple-element.7), kind=kLoop, calls=%fused_computation.82 | loop fusion | flops 1966080 | bytes 7864320 | tf_op jit(solution)/shard_map/add | solution.py:89
  102.4 0.2 copy-done.16
  102.7 5.4 %fusion.3 = f32[512,1536]{1,0:T(8,128)S(1)} fusion(f32[512,768]{1,0:T(8,128)S(1)} %multiply_add_fusion.2, f32[512,768]{1,0:T(8,128)S(1)} %copy-done.16, f32[256,512]{1,0:T(8,128)S(1)} %copy-done.11, f32[256,512]{1,0:T(8,128)S(1)} %copy-done.9), kind=kOutput, calls=%fused_computation.7 | convolution fusion | flops 4832886784 | bytes 7340032 | tf_op jit(solution)/shard_map/dot_general | solution.py:47
  108.1 0.0 copy-start.27
  108.1 0.2 slice_subtract_fusion.6
  108.3 1.2 copy-done.3
  109.5 0.1 copy-done.27
  109.6 3.7 %multiply_reduce_fusion.1 = (f32[]{:T(128)}, f32[256,512]{1,0:T(8,128)S(1)}) fusion(f32[256,512]{1,0:T(8,128)S(1)} %copy-done.27, f32[512,768]{1,0:T(8,128)S(1)} %get-tuple-element.29, f32[512,768]{1,0:T(8,128)S(1)} %copy-done.3, f32[256,768]{1,0:T(8,128)S(1)} %get-tuple-element.18, f32[256,768]{1,0:T(8,128)S(1)} %get-tuple-element.17), kind=kOutput, calls=%fused_computation.139 | convolution fusion | flops 2417623040 | bytes 5767172 | tf_op jit(solution)/shard_map/dot_general | solution.py:54
  113.4 2.8 %fusion.2 = f32[256,1536]{1,0:T(8,128)S(1)} fusion(f32[256,512]{1,0:T(8,128)S(1)} %get-tuple-element.38, f32[512,768]{1,0:T(8,128)S(1)} %get-tuple-element.29, f32[512,768]{1,0:T(8,128)S(1)} %copy-done.17), kind=kOutput, calls=%fused_computation.6 | convolution fusion | flops 2416705536 | bytes 5242880 | tf_op jit(solution)/shard_map/dot_general | solution.py:35
  116.2 5.6 %fusion.71 = f32[1024,1536]{1,0:T(8,128)S(1)} fusion(f32[256,1536]{1,0:T(8,128)S(1)} %fusion.2, f32[256,512]{1,0:T(8,128)S(1)} %copy-done.11, f32[256,512]{1,0:T(8,128)S(1)} %copy-done.9), kind=kOutput, calls=%fused_computation.100 | convolution fusion | flops 4832100352 | bytes 8912896 | tf_op jit(solution)/shard_map/dot_general | solution.py:36
  121.8 1.3 collective-permute-start.4
  123.1 1.8 collective-permute-start.5
  125.0 0.6 multiply_add_fusion
  125.6 5.4 %fusion.12 = f32[512,1536]{1,0:T(8,128)S(1)} fusion(f32[512,768]{1,0:T(8,128)S(1)} %get-tuple-element.10, f32[512,768]{1,0:T(8,128)S(1)} %get-tuple-element.9, f32[256,512]{1,0:T(8,128)S(1)} %copy-done.23, f32[256,512]{1,0:T(8,128)S(1)} %copy-done.21), kind=kOutput, calls=%fused_computation.16 | convolution fusion | flops 4832886784 | bytes 7340032 | tf_op jit(solution)/shard_map/dot_general | solution.py:47
  131.1 0.9 pad_maximum_fusion.26
  132.0 4.2 %collective-permute-start.6 = (f32[512,128]{1,0:T(8,128)}, f32[512,128]{1,0:T(8,128)}, u32[]{:S(2)}, u32[]{:S(2)}) collective-permute-start(f32[512,128]{1,0:T(8,128)} %get-tuple-element.19), channel_id=1, source_target_pairs={{0,1},{1,2},{2,3},{4,5},{5,6},{6,7},{8,9},{9,10},{10,11},{12,13},{... | collective-permute-start | bytes 786440 | tf_op jit(solution)/shard_map/ppermute | solution.py:16
  136.1 1.4 collective-permute-start.7
  137.5 0.2 slice_subtract_fusion.4
  137.8 2.2 fusion.91
  139.9 0.0 reduce-scatter.2.cloned.1.call-update
  140.0 0.0 all-reduce.3.cloned.1.call-start
  140.0 0.4 collective-permute-done.6
  140.4 5.5 %collective-permute-done.7 = f32[512,128]{1,0:T(8,128)} collective-permute-done((f32[512,128]{1,0:T(8,128)}, f32[512,128]{1,0:T(8,128)}, u32[]{:S(2)}, u32[]{:S(2)}) %collective-permute-start.7) | collective-permute-done | bytes 262176 | tf_op jit(solution)/shard_map/ppermute | solution.py:19
  145.9 10.4 %fusion = f32[512,1536]{1,0:T(8,128)S(1)} fusion(f32[768,768]{1,0:T(8,128)} %copy-done.25, f32[768,768]{1,0:T(8,128)} %copy-done.26, f32[512,128]{1,0:T(8,128)} %collective-permute-done.7, f32[128,512]{1,0:T(8,128)} %copy-done.29, f32[256,512]{1,0:T(8,128)} %copy-done.13, f32[128,512]{1,0:T(8,128)S(1)} %collective-permute-done.4, ...), kind=kOutput, calls=%fused_computation.1 | convolution fusion | flops 7250509824 | bytes 9437184 | tf_op jit(solution)/shard_map/dot_general | solution.py:35
  156.4 10.9 %fusion.25 = f32[1024,1536]{1,0:T(8,128)S(1)} fusion(f32[512,1536]{1,0:T(8,128)S(1)} %fusion, f32[512,512]{1,0:T(8,128)S(1)} %copy-done.6, f32[512,512]{1,0:T(8,128)S(1)} %copy-done.8), kind=kOutput, calls=%fused_computation.34 | convolution fusion | flops 9664200704 | bytes 11534336 | tf_op jit(solution)/shard_map/dot_general | solution.py:36
  167.3 0.0 copy-start.10
  167.3 0.8 multiply_add_fusion.1
  168.1 0.2 copy-done.10
  168.4 0.2 copy-done.12
  168.5 5.6 %fusion.7 = f32[512,1536]{1,0:T(8,128)S(1)} fusion(f32[512,768]{1,0:T(8,128)S(1)} %get-tuple-element.12, f32[512,768]{1,0:T(8,128)S(1)} %get-tuple-element.11, f32[256,512]{1,0:T(8,128)S(1)} %copy-done.12, f32[256,512]{1,0:T(8,128)S(1)} %copy-done.10), kind=kOutput, calls=%fused_computation.11 | convolution fusion | flops 4832886784 | bytes 7340032 | tf_op jit(solution)/shard_map/dot_general | solution.py:47
  174.1 0.2 slice_subtract_fusion.5
  174.3 1.2 copy-done.4
  175.5 3.5 %multiply_reduce_fusion = (f32[]{:T(128)}, f32[256,512]{1,0:T(8,128)S(1)}) fusion(f32[512,768]{1,0:T(8,128)S(1)} %get-tuple-element.29, f32[512,768]{1,0:T(8,128)S(1)} %copy-done.4, f32[256,768]{1,0:T(8,128)S(1)} %get-tuple-element.16, f32[256,768]{1,0:T(8,128)S(1)} %get-tuple-element.15), kind=kOutput, calls=%fused_computation.138 | convolution fusion | flops 2417491968 | bytes 5242884 | tf_op jit(solution)/shard_map/dot_general | solution.py:54
  179.0 31.2 %all-reduce = (f32[]{:T(128)}, f32[]{:T(128)}) all-reduce(f32[]{:T(128)} %get-tuple-element.37, f32[]{:T(128)} %get-tuple-element.39), channel_id=1, replica_groups=mesh['groups'=2,'row'=4,'col'=4] {'row','col'}, use_global_device_ids=true, to_apply=%region_1.2 | all-reduce | flops 2 | bytes 16 | tf_op jit(solution)/shard_map/psum | solution.py:97
  211.6 0.0 reduce-scatter.2.cloned.1.call-done
  211.6 0.0 all-reduce.3.cloned.1.call-update
  211.6 0.9 multiply_subtract_fusion.3
  212.5 34.5 %all-reduce.3.cloned.1.call-done = f32[64,256]{1,0:T(8,128)} async-done(((f32[64,256]{1,0:T(8,128)}), f32[64,256]{1,0:T(8,128)}) %all-reduce.3.cloned.1.call-update) | async-done | bytes 65552 | tf_op jit(solution)/shard_map/psum | solution.py:122
  247.0 1.4 multiply_reduce_fusion.2
  249.1 6.2 %psum.31 = f32[]{:T(128)} all-reduce(f32[]{:T(128)} %multiply_reduce_fusion.2), channel_id=1, replica_groups=mesh['groups'=2,'row'=4,'col'=4] {'row'}, use_global_device_ids=true, to_apply=%region_7.8 | all-reduce | flops 1 | bytes 8 | tf_op jit(solution)/shard_map/psum | solution.py:123
  256.0 1.5 multiply_subtract_fusion.4
  (61 shorter events, 0.3 us)
Async XLA Ops:
  7.2 204.4 %reduce-scatter.2.cloned.1.call-start = ((), (), s32[]{:S(2)}) async-start(), calls=%async_computation.1 | async-start | bytes 327680 | tf_op jit(solution)/shard_map/reduce_scatter | solution.py:121
  8.3 55.3 %collective-permute-start = (f32[128,512]{1,0:T(8,128)S(1)}, f32[128,512]{1,0:T(8,128)S(1)}, u32[]{:S(2)}, u32[]{:S(2)}) collective-permute-start(f32[128,512]{1,0:T(8,128)S(1)} %get-tuple-element.26), channel_id=1, source_target_pairs={{0,4},{4,8},{8,12},{1,5},{5,9},{9,13},{2,6},{6,10},{10,14},{3,7},{... | collective-permute-start | bytes 786440 | tf_op jit(solution)/shard_map/ppermute | solution.py:16
  10.7 53.0 %collective-permute-start.1 = (f32[128,512]{1,0:T(8,128)S(1)}, f32[128,512]{1,0:T(8,128)S(1)}, u32[]{:S(2)}, u32[]{:S(2)}) collective-permute-start(f32[128,512]{1,0:T(8,128)S(1)} %get-tuple-element.25), channel_id=1, source_target_pairs={{4,0},{8,4},{12,8},{5,1},{9,5},{13,9},{6,2},{10,6},{14,10},{7,3},{... | collective-permute-start | bytes 786440 | tf_op jit(solution)/shard_map/ppermute | solution.py:19
  12.0 6.4 %copy-start.28 = (f32[64,256]{1,0:T(8,128)S(1)}, f32[64,256]{1,0:T(8,128)}, u32[]{:S(2)}) copy-start(f32[64,256]{1,0:T(8,128)} %param.5) | copy-start | bytes 196612
  16.2 19.6 %copy-start.14 = (f32[256,768]{1,0:T(8,128)}, f32[256,768]{1,0:T(8,128)S(1)}, u32[]{:S(2)}) copy-start(f32[256,768]{1,0:T(8,128)S(1)} %get-tuple-element.32) | copy-start | bytes 2359300
  18.4 20.2 %copy-start.20 = (f32[256,512]{1,0:T(8,128)}, f32[256,512]{1,0:T(8,128)S(1)}, u32[]{:S(2)}) copy-start(f32[256,512]{1,0:T(8,128)S(1)} %get-tuple-element.35) | copy-start | bytes 1572868
  18.4 20.2 %copy-start.22 = (f32[256,512]{1,0:T(8,128)}, f32[256,512]{1,0:T(8,128)S(1)}, u32[]{:S(2)}) copy-start(f32[256,512]{1,0:T(8,128)S(1)} %get-tuple-element.36) | copy-start | bytes 1572868
  59.1 18.4 %copy-start.25 = (f32[768,768]{1,0:T(8,128)}, f32[768,768]{1,0:T(8,128)S(1)}, u32[]{:S(2)}) copy-start(f32[768,768]{1,0:T(8,128)S(1)} %get-tuple-element.41) | copy-start | bytes 7077892
  59.1 18.4 %copy-start.26 = (f32[768,768]{1,0:T(8,128)}, f32[768,768]{1,0:T(8,128)S(1)}, u32[]{:S(2)}) copy-start(f32[768,768]{1,0:T(8,128)S(1)} %get-tuple-element.42) | copy-start | bytes 7077892
  59.1 4.6 %copy-start.18 = (f32[256,512]{1,0:T(8,128)S(1)}, f32[256,512]{1,0:T(8,128)}, u32[]{:S(2)}) copy-start(f32[256,512]{1,0:T(8,128)} %param.4) | copy-start | bytes 1572868
  63.6 21.6 %copy-start.5 = (f32[512,512]{1,0:T(8,128)}, f32[512,512]{1,0:T(8,128)S(1)}, u32[]{:S(2)}) copy-start(f32[512,512]{1,0:T(8,128)S(1)} %get-tuple-element.43) | copy-start | bytes 3145732
  63.6 21.6 %copy-start.7 = (f32[512,512]{1,0:T(8,128)}, f32[512,512]{1,0:T(8,128)S(1)}, u32[]{:S(2)}) copy-start(f32[512,512]{1,0:T(8,128)S(1)} %get-tuple-element.44) | copy-start | bytes 3145732
  63.8 9.5 %collective-permute-start.2 = (f32[512,128]{1,0:T(8,128)S(1)}, f32[512,128]{1,0:T(8,128)S(1)}, u32[]{:S(2)}, u32[]{:S(2)}) collective-permute-start(f32[512,128]{1,0:T(8,128)S(1)} %get-tuple-element.21), channel_id=1, source_target_pairs={{0,1},{1,2},{2,3},{4,5},{5,6},{6,7},{8,9},{9,10},{10,11},{12,13},{... | collective-permute-start | bytes 786440 | tf_op jit(solution)/shard_map/ppermute | solution.py:16
  67.3 10.2 %collective-permute-start.3 = (f32[512,128]{1,0:T(8,128)S(1)}, f32[512,128]{1,0:T(8,128)S(1)}, u32[]{:S(2)}, u32[]{:S(2)}) collective-permute-start(f32[512,128]{1,0:T(8,128)S(1)} %get-tuple-element.22), channel_id=1, source_target_pairs={{1,0},{2,1},{3,2},{5,4},{6,5},{7,6},{9,8},{10,9},{11,10},{13,12},{... | collective-permute-start | bytes 786440 | tf_op jit(solution)/shard_map/ppermute | solution.py:19
  99.5 2.9 %copy-start.9 = (f32[256,512]{1,0:T(8,128)S(1)}, f32[256,512]{1,0:T(8,128)}, u32[]{:S(2)}) copy-start(f32[256,512]{1,0:T(8,128)} %get-tuple-element.33) | copy-start | bytes 1572868
  99.5 2.9 %copy-start.11 = (f32[256,512]{1,0:T(8,128)S(1)}, f32[256,512]{1,0:T(8,128)}, u32[]{:S(2)}) copy-start(f32[256,512]{1,0:T(8,128)} %get-tuple-element.34) | copy-start | bytes 1572868
  99.5 3.1 %copy-start.16 = (f32[512,768]{1,0:T(8,128)S(1)}, f32[512,768]{1,0:T(8,128)}, u32[]{:S(2)}) copy-start(f32[512,768]{1,0:T(8,128)} %get-tuple-element.4) | copy-start | bytes 4718596
  108.1 1.4 copy-start.3
  108.1 1.5 copy-start.27
  109.6 3.8 %copy-start.17 = (f32[512,768]{1,0:T(8,128)S(1)}, f32[512,768]{1,0:T(8,128)}, u32[]{:S(2)}) copy-start(f32[512,768]{1,0:T(8,128)} %get-tuple-element.27) | copy-start | bytes 4718596
  113.3 17.7 %copy-start.13 = (f32[256,512]{1,0:T(8,128)}, f32[256,512]{1,0:T(8,128)S(1)}, u32[]{:S(2)}) copy-start(f32[256,512]{1,0:T(8,128)S(1)} %get-tuple-element.38) | copy-start | bytes 1572868
  116.2 8.8 %copy-start.1 = (f32[512,768]{1,0:T(8,128)S(1)}, f32[512,768]{1,0:T(8,128)}, u32[]{:S(2)}) copy-start(f32[512,768]{1,0:T(8,128)} %get-tuple-element.5) | copy-start | bytes 4718596
  116.2 8.8 %copy-start.2 = (f32[512,768]{1,0:T(8,128)S(1)}, f32[512,768]{1,0:T(8,128)}, u32[]{:S(2)}) copy-start(f32[512,768]{1,0:T(8,128)} %get-tuple-element.6) | copy-start | bytes 4718596
  121.8 9.2 %collective-permute-start.4 = (f32[128,512]{1,0:T(8,128)S(1)}, f32[128,512]{1,0:T(8,128)S(1)}, u32[]{:S(2)}, u32[]{:S(2)}) collective-permute-start(f32[128,512]{1,0:T(8,128)S(1)} %get-tuple-element.23), channel_id=1, source_target_pairs={{0,4},{4,8},{8,12},{1,5},{5,9},{9,13},{2,6},{6,10},{10,14},{3,7},{... | collective-permute-start | bytes 786440 | tf_op jit(solution)/shard_map/ppermute | solution.py:16
  123.1 2.5 copy-start.21
  123.1 2.5 copy-start.23
  123.1 7.9 %collective-permute-start.5 = (f32[128,512]{1,0:T(8,128)S(1)}, f32[128,512]{1,0:T(8,128)S(1)}, u32[]{:S(2)}, u32[]{:S(2)}) collective-permute-start(f32[128,512]{1,0:T(8,128)S(1)} %get-tuple-element.24), channel_id=1, source_target_pairs={{4,0},{8,4},{12,8},{5,1},{9,5},{13,9},{6,2},{10,6},{14,10},{7,3},{... | collective-permute-start | bytes 786440 | tf_op jit(solution)/shard_map/ppermute | solution.py:19
  131.0 6.7 %copy-start.29 = (f32[128,512]{1,0:T(8,128)}, f32[128,512]{1,0:T(8,128)S(1)}, u32[]{:S(2)}) copy-start(f32[128,512]{1,0:T(8,128)S(1)} %collective-permute-done.5) | copy-start | bytes 786436
  132.0 8.5 %collective-permute-start.6 = (f32[512,128]{1,0:T(8,128)}, f32[512,128]{1,0:T(8,128)}, u32[]{:S(2)}, u32[]{:S(2)}) collective-permute-start(f32[512,128]{1,0:T(8,128)} %get-tuple-element.19), channel_id=1, source_target_pairs={{0,1},{1,2},{2,3},{4,5},{5,6},{6,7},{8,9},{9,10},{10,11},{12,13},{... | collective-permute-start | bytes 786440 | tf_op jit(solution)/shard_map/ppermute | solution.py:16
  136.1 1.6 copy-start.15
  136.1 1.6 copy-start.24
  136.1 9.8 %collective-permute-start.7 = (f32[512,128]{1,0:T(8,128)}, f32[512,128]{1,0:T(8,128)}, u32[]{:S(2)}, u32[]{:S(2)}) collective-permute-start(f32[512,128]{1,0:T(8,128)} %get-tuple-element.20), channel_id=1, source_target_pairs={{1,0},{2,1},{3,2},{5,4},{6,5},{7,6},{9,8},{10,9},{11,10},{13,12},{... | collective-permute-start | bytes 786440 | tf_op jit(solution)/shard_map/ppermute | solution.py:19
  140.0 107.1 %all-reduce.3.cloned.1.call-start = ((), (), s32[]{:S(2)}) async-start(), calls=%async_computation.2 | async-start | bytes 131072 | tf_op jit(solution)/shard_map/psum | solution.py:122
  140.0 16.3 %copy-start.6 = (f32[512,512]{1,0:T(8,128)S(1)}, f32[512,512]{1,0:T(8,128)}, u32[]{:S(2)}) copy-start(f32[512,512]{1,0:T(8,128)} %copy-done.5) | copy-start | bytes 3145732
  140.0 16.3 %copy-start.8 = (f32[512,512]{1,0:T(8,128)S(1)}, f32[512,512]{1,0:T(8,128)}, u32[]{:S(2)}) copy-start(f32[512,512]{1,0:T(8,128)} %copy-done.7) | copy-start | bytes 3145732
  156.4 10.9 %copy-start = (f32[512,768]{1,0:T(8,128)S(1)}, f32[512,768]{1,0:T(8,128)}, u32[]{:S(2)}) copy-start(f32[512,768]{1,0:T(8,128)} %get-tuple-element.8) | copy-start | bytes 4718596
  167.3 1.0 copy-start.10
  167.3 1.2 copy-start.12
  174.1 1.4 copy-start.4
  175.5 36.1 %copy-start.19 = (f32[256,512]{1,0:T(8,128)S(1)}, f32[256,512]{1,0:T(8,128)}, u32[]{:S(2)}) copy-start(f32[256,512]{1,0:T(8,128)} %param.4) | copy-start | bytes 1572868
Sparse Core Ops, SparseCore 0:
  140.1 23.7 reduce-scatter.1
  211.7 35.2 all-reduce.2
where the time goes:
time: 269 us; the launch traced here: 265 us
  matrix products  88.1 us (33%)
  blocking collectives  46.5 us (17%)
  waiting for transfers between devices  46.1 us (17%)
  other arithmetic  44.6 us (17%)
  between operations  17.6 us (7%)
  starting transfers between devices  17.2 us (6%)
  local copies, waits for them, and re-layouts  4.45 us (2%)
    dot_general x4, matrix products, forward(): lax.dot_general(jnp.concatenate(row_tables, 1), across, (((0,), (0,)), ((...  38.7 us
    psum x1, waiting for transfers between devices, per_device(): owner_grad = lax.psum(owner_grad, 'col')  34.5 us
    psum x1, blocking collectives, per_device(): loss = 0.5 * lax.psum(local_squares, ('row', 'col'))  31.2 us
    dot_general x4, matrix products, forward(): across = jnp.dot(field, jnp.concatenate(col_tables, 1), precision=HIGHEST)  23.6 us
    sin x3, other arithmetic, tables(): return (jnp.cos(phase), jnp.sin(phase))  22.3 us
    dot_general x3, matrix products, inverse(): jnp.dot(jnp.concatenate(row_tables, 0), jnp.concatenate([real_part, imag_...  16.4 us
    ppermute x4, starting transfers between devices, padded(): lax.ppermute(lax.slice_in_dim(block, block.shape[dim] - width, None, axis...  11.3 us
    ppermute x4, waiting for transfers between devices, padded(): lax.ppermute(lax.slice_in_dim(block, 0, width, axis=dim), axis, backward)  9.63 us
  transfers between devices with their start and end apart: 10, of which 5 were waited for; matrix products, arithmetic and copies ran while one was open for 33% of the time, Pallas kernels for 0%

commit v1 on v0

--- a/solution.py
+++ b/solution.py
@@ -119,7 +119,8 @@
     grad_squares = jnp.sum(image_grad * image_grad)
     image_norm = lax.psum(grad_squares, ("row", "col"))
     owner_grad = lax.psum_scatter(kernel_grad, "row", scatter_dimension=0, tiled=True)
-    owner_grad = lax.psum(owner_grad, "col")
+    mid_arr = jax.lax.all_gather(owner_grad, "col")
+    owner_grad = jnp.sum(mid_arr, axis=0)
     kernel_norm = lax.psum(jnp.sum(owner_grad * owner_grad), "row")
     owned = owned - 0.25 * loss / (kernel_norm + EPSILON) * owner_grad
     image = image - loss / (image_norm + EPSILON) * image_grad

time: 269 us -> 260 us (0.967)
  waiting for transfers between devices: 46.1 us -> 14.4 us
  blocking collectives: 46.5 us -> 63.2 us
  matrix products: 88.1 us -> 90.9 us
    psum x1 -> x0, waiting for transfers between devices: 34.5 us -> none  [per_device(): owner_grad = lax.psum(owner_grad, 'col')]
    all_gather x0 -> x1, blocking collectives: none -> 14.5 us  [per_device(): mid_arr = jax.lax.all_gather(owner_grad, 'col')]
    reduce_scatter x1, waiting for transfers between devices: 0.02 us -> 4.9 us  [per_device(): lax.psum_scatter(kernel_grad, 'row', scatter_dimension=0, tiled=True)]
  transfers between devices with their start and end apart: 10 -> 9, of which waited for: 5 -> 4; matrix products, arithmetic and copies ran while one was open for 33% -> 19% of each run, Pallas kernels for 0% -> 0%
where the time goes in v1:
time: 260 us; the launch traced here: 255 us
  matrix products  90.9 us (35%)
  blocking collectives  63.2 us (24%)
  other arithmetic  46.2 us (18%)
  between operations  17.4 us (7%)
  starting transfers between devices  16.5 us (6%)
  waiting for transfers between devices  14.4 us (6%)
  local copies, waits for them, and re-layouts  6.69 us (3%)
    dot_general x4, matrix products, forward(): lax.dot_general(jnp.concatenate(row_tables, 1), across, (((0,), (0,)), ((...  38.7 us
    psum x1, blocking collectives, per_device(): loss = 0.5 * lax.psum(local_squares, ('row', 'col'))  33.3 us
    dot_general x4, matrix products, forward(): across = jnp.dot(field, jnp.concatenate(col_tables, 1), precision=HIGHEST)  23.9 us
    sin x3, other arithmetic, tables(): return (jnp.cos(phase), jnp.sin(phase))  22.3 us
    dot_general x3, matrix products, inverse(): jnp.dot(jnp.concatenate(row_tables, 0), jnp.concatenate([real_part, imag_...  16.8 us
    all_gather x1, blocking collectives, per_device(): mid_arr = jax.lax.all_gather(owner_grad, 'col')  14.5 us
    dot_general x3, matrix products, inverse(): lax.dot_general(jnp.concatenate([mixed_re, mixed_im], 1), jnp.concatenate...  11.5 us
    ppermute x4, starting transfers between devices, padded(): lax.ppermute(lax.slice_in_dim(block, block.shape[dim] - width, None, axis...  11.3 us
  transfers between devices with their start and end apart: 9, of which 4 were waited for; matrix products, arithmetic and copies ran while one was open for 19% of the time, Pallas kernels for 0%

profile of v1, /device:TPU:0, one launch (start us, length us, event | category | flops | bytes accessed | tf_op | source)
XLA Modules:
  0.0 255.4 jit_solution(3134599679292049373)
XLA Ops:
  7.2 0.0 reduce-scatter.2.cloned.1.call-start
  7.2 1.1 fusion.130
  8.3 2.4 collective-permute-start
  10.7 1.3 collective-permute-start.1
  12.0 0.0 copy-start.27
  12.0 4.2 %fusion.109 = (f32[256,768]{1,0:T(8,128)}, f32[256,768]{1,0:T(8,128)S(1)}, f32[256,768]{1,0:T(8,128)S(1)}) fusion(s32[256]{0:T(256)S(1)} %iota_add_fusion.1), kind=kLoop, calls=%fused_computation.148 | loop fusion | flops 1966080 | bytes 2360320 | tf_op jit(solution)/shard_map/neg | solution.py:56
  16.2 2.1 fusion.111
  18.4 9.1 %all_gather.9 = f32[256,256]{1,0:T(8,128)S(1)} all-gather(f32[64,256]{1,0:T(8,128)S(1)} %copy-done.27), channel_id=1, replica_groups=mesh['groups'=2,'row'=4,'col'=4] {'row'}, dimensions={0}, use_global_device_ids=true | all-gather | bytes 327680 | tf_op jit(solution)/shard_map/all_gather | solution.py:64
  27.5 8.3 %fusion.58 = (f32[512,768]{1,0:T(8,128)}, f32[512,768]{1,0:T(8,128)}, f32[512,768]{1,0:T(8,128)S(1)}) fusion(s32[512]{0:T(512)S(1)} %iota_add_fusion), kind=kLoop, calls=%fused_computation.80 | loop fusion | flops 3932160 | bytes 4720640 | tf_op jit(solution)/shard_map/sin | solution.py:29
  35.8 2.7 %fusion.27 = f32[1536,256]{1,0:T(8,128)S(1)} fusion(f32[256,256]{1,0:T(8,128)S(1)} %all_gather.9, f32[256,768]{1,0:T(8,128)S(1)} %get-tuple-element.32, f32[256,768]{1,0:T(8,128)S(1)} %get-tuple-element.31), kind=kOutput, calls=%fused_computation.36 | convolution fusion | flops 1208352768 | bytes 3407872 | tf_op jit(solution)/shard_map/dot_general | solution.py:35
  38.6 11.0 %fusion.64 = f32[1024,1536]{1,0:T(8,128)S(1)} fusion(f32[1536,256]{1,0:T(8,128)S(1)} %fusion.27, f32[256,512]{1,0:T(8,128)S(1)} %get-tuple-element.36, f32[256,512]{1,0:T(8,128)S(1)} %get-tuple-element.35), kind=kOutput, calls=%fused_computation.93 | convolution fusion | flops 4832100352 | bytes 8912896 | tf_op jit(solution)/shard_map/dot_general | solution.py:36
  49.6 9.5 %fusion.22 = (f32[768,768]{1,0:T(8,128)S(1)}, f32[768,768]{1,0:T(8,128)S(1)}) fusion(), kind=kLoop, calls=%fused_computation.28 | loop fusion | flops 5308416 | bytes 4718592 | tf_op jit(solution)/shard_map/sin | solution.py:29
  59.1 0.0 copy-start.18
  59.1 4.5 %fusion.103 = (f32[512,512]{1,0:T(8,128)S(1)}, f32[512,512]{1,0:T(8,128)S(1)}) fusion(), kind=kLoop, calls=%fused_computation.142 | loop fusion | flops 3670016 | bytes 2097152 | tf_op jit(solution)/shard_map/sin | solution.py:29
  63.8 3.5 %collective-permute-start.2 = (f32[512,128]{1,0:T(8,128)S(1)}, f32[512,128]{1,0:T(8,128)S(1)}, u32[]{:S(2)}, u32[]{:S(2)}) collective-permute-start(f32[512,128]{1,0:T(8,128)S(1)} %get-tuple-element.21), channel_id=1, source_target_pairs={{0,1},{1,2},{2,3},{4,5},{5,6},{6,7},{8,9},{9,10},{10,11},{12,13},{... | collective-permute-start | bytes 786440 | tf_op jit(solution)/shard_map/ppermute | solution.py:16
  67.3 1.3 collective-permute-start.3
  68.6 3.2 %fusion.113 = (f32[256,512]{1,0:T(8,128)}, f32[256,512]{1,0:T(8,128)}) fusion(s32[256]{0:T(256)S(1)} %iota_add_fusion.2), kind=kLoop, calls=%fused_computation.155 | loop fusion | flops 1835008 | bytes 1049600 | tf_op jit(solution)/shard_map/cos | solution.py:29
  71.8 1.5 collective-permute-done.2
  73.3 4.1 %collective-permute-done.3 = f32[512,128]{1,0:T(8,128)S(1)} collective-permute-done((f32[512,128]{1,0:T(8,128)S(1)}, f32[512,128]{1,0:T(8,128)S(1)}, u32[]{:S(2)}, u32[]{:S(2)}) %collective-permute-start.3) | collective-permute-done | bytes 262176 | tf_op jit(solution)/shard_map/ppermute | solution.py:19
  77.5 7.7 %fusion.1 = f32[512,1536]{1,0:T(8,128)S(1)} fusion(f32[768,768]{1,0:T(8,128)S(1)} %get-tuple-element.41, f32[768,768]{1,0:T(8,128)S(1)} %get-tuple-element.42, f32[512,128]{1,0:T(8,128)S(1)} %collective-permute-done.3, f32[512,512]{1,0:T(8,128)S(1)} %constant_dynamic-update-slice_fusion, f32[512,128]{1,0:T(8,128)S(1)} %collective-permute-done.2), kind=kOutput, calls=%fused_computation.2 | convolution fusion | flops 7249723392 | bytes 9437184 | tf_op jit(solution)/shard_map/dot_general | solution.py:35
  85.2 11.2 %fusion.26 = f32[1024,1536]{1,0:T(8,128)S(1)} fusion(f32[512,1536]{1,0:T(8,128)S(1)} %fusion.1, f32[512,512]{1,0:T(8,128)S(1)} %get-tuple-element.43, f32[512,512]{1,0:T(8,128)S(1)} %get-tuple-element.44), kind=kOutput, calls=%fused_computation.35 | convolution fusion | flops 9664200704 | bytes 11534336 | tf_op jit(solution)/shard_map/dot_general | solution.py:36
  96.4 3.1 %multiply_subtract_fusion.2 = (f32[512,768]{1,0:T(8,128)}, f32[512,768]{1,0:T(8,128)}, f32[512,768]{1,0:T(8,128)}, f32[512,768]{1,0:T(8,128)S(1)}, f32[512,768]{1,0:T(8,128)}) fusion(f32[1024,1536]{1,0:T(8,128)S(1)} %fusion.26, f32[1024,1536]{1,0:T(8,128)S(1)} %fusion.64), kind=kLoop, calls=%fused_computation.83 | loop fusion | flops 2752512 | bytes 20447232 | tf_op jit(solution)/shard_map/sub | solution.py:88
  99.5 2.9 %multiply_add_fusion.2 = f32[512,768]{1,0:T(8,128)S(1)} fusion(f32[512,768]{1,0:T(8,128)} %get-tuple-element.8, f32[512,768]{1,0:T(8,128)} %get-tuple-element.6, f32[512,768]{1,0:T(8,128)} %get-tuple-element.5, f32[512,768]{1,0:T(8,128)S(1)} %get-tuple-element.7), kind=kLoop, calls=%fused_computation.82 | loop fusion | flops 1966080 | bytes 7864320 | tf_op jit(solution)/shard_map/add | solution.py:89
  102.4 0.2 copy-done.16
  102.7 5.4 %fusion.3 = f32[512,1536]{1,0:T(8,128)S(1)} fusion(f32[512,768]{1,0:T(8,128)S(1)} %multiply_add_fusion.2, f32[512,768]{1,0:T(8,128)S(1)} %copy-done.16, f32[256,512]{1,0:T(8,128)S(1)} %copy-done.11, f32[256,512]{1,0:T(8,128)S(1)} %copy-done.9), kind=kOutput, calls=%fused_computation.7 | convolution fusion | flops 4832886784 | bytes 7340032 | tf_op jit(solution)/shard_map/dot_general | solution.py:47
  108.0 0.0 copy-start.26
  108.1 0.2 slice_subtract_fusion.6
  108.2 1.2 copy-done.3
  109.4 0.1 copy-done.26
  109.5 3.7 %multiply_reduce_fusion.1 = (f32[]{:T(128)}, f32[256,512]{1,0:T(8,128)S(1)}) fusion(f32[256,512]{1,0:T(8,128)S(1)} %copy-done.26, f32[512,768]{1,0:T(8,128)S(1)} %get-tuple-element.29, f32[512,768]{1,0:T(8,128)S(1)} %copy-done.3, f32[256,768]{1,0:T(8,128)S(1)} %get-tuple-element.18, f32[256,768]{1,0:T(8,128)S(1)} %get-tuple-element.17), kind=kOutput, calls=%fused_computation.139 | convolution fusion | flops 2417623040 | bytes 5767172 | tf_op jit(solution)/shard_map/dot_general | solution.py:54
  113.3 2.8 %fusion.2 = f32[256,1536]{1,0:T(8,128)S(1)} fusion(f32[256,512]{1,0:T(8,128)S(1)} %get-tuple-element.38, f32[512,768]{1,0:T(8,128)S(1)} %get-tuple-element.29, f32[512,768]{1,0:T(8,128)S(1)} %copy-done.17), kind=kOutput, calls=%fused_computation.6 | convolution fusion | flops 2416705536 | bytes 5242880 | tf_op jit(solution)/shard_map/dot_general | solution.py:35
  116.1 5.6 %fusion.71 = f32[1024,1536]{1,0:T(8,128)S(1)} fusion(f32[256,1536]{1,0:T(8,128)S(1)} %fusion.2, f32[256,512]{1,0:T(8,128)S(1)} %copy-done.11, f32[256,512]{1,0:T(8,128)S(1)} %copy-done.9), kind=kOutput, calls=%fused_computation.100 | convolution fusion | flops 4832100352 | bytes 8912896 | tf_op jit(solution)/shard_map/dot_general | solution.py:36
  121.8 0.6 multiply_add_fusion
  122.4 0.4 copy-done.20
  122.8 0.2 copy-done.22
  122.9 5.8 %fusion.12 = f32[512,1536]{1,0:T(8,128)S(1)} fusion(f32[512,768]{1,0:T(8,128)S(1)} %get-tuple-element.10, f32[512,768]{1,0:T(8,128)S(1)} %get-tuple-element.9, f32[256,512]{1,0:T(8,128)S(1)} %copy-done.22, f32[256,512]{1,0:T(8,128)S(1)} %copy-done.20), kind=kOutput, calls=%fused_computation.16 | convolution fusion | flops 4832886784 | bytes 7340032 | tf_op jit(solution)/shard_map/dot_general | solution.py:47
  128.8 0.2 slice_subtract_fusion.4
  129.0 0.9 copy-done.15
  129.9 0.2 copy-done.23
  130.1 2.2 fusion.91
  132.3 0.0 reduce-scatter.2.cloned.1.call-update
  132.3 1.1 fusion.129
  133.4 1.3 collective-permute-start.4
  134.7 1.3 collective-permute-start.5
  136.0 3.9 %collective-permute-done.5 = f32[128,512]{1,0:T(8,128)S(1)} collective-permute-done((f32[128,512]{1,0:T(8,128)S(1)}, f32[128,512]{1,0:T(8,128)S(1)}, u32[]{:S(2)}, u32[]{:S(2)}) %collective-permute-start.5) | collective-permute-done | bytes 262176 | tf_op jit(solution)/shard_map/ppermute | solution.py:19
  139.9 0.7 copy-done.29
  140.6 1.8 pad_maximum_fusion.26
  142.4 4.1 %collective-permute-start.6 = (f32[512,128]{1,0:T(8,128)}, f32[512,128]{1,0:T(8,128)}, u32[]{:S(2)}, u32[]{:S(2)}) collective-permute-start(f32[512,128]{1,0:T(8,128)} %get-tuple-element.19), channel_id=1, source_target_pairs={{0,1},{1,2},{2,3},{4,5},{5,6},{6,7},{8,9},{9,10},{10,11},{12,13},{... | collective-permute-start | bytes 786440 | tf_op jit(solution)/shard_map/ppermute | solution.py:16
  146.5 1.3 collective-permute-start.7
  147.8 4.9 %reduce-scatter.2.cloned.1.call-done = f32[64,256]{1,0:T(8,128)} async-done(((f32[256,256]{1,0:T(8,128)}), f32[64,256]{1,0:T(8,128)}) %reduce-scatter.2.cloned.1.call-update) | async-done | bytes 65552 | tf_op jit(solution)/shard_map/reduce_scatter | solution.py:121
  152.7 14.5 %all-gather = f32[256,256]{1,0:T(8,128)S(1)} all-gather(f32[64,256]{1,0:T(8,128)} %reduce-scatter.2.cloned.1.call-done), channel_id=2, replica_groups=mesh['groups'=2,'row'=4,'col'=4] {'col'}, dimensions={0}, use_global_device_ids=true | all-gather | bytes 327680 | tf_op jit(solution)/shard_map/all_gather | solution.py:122
  167.2 0.7 multiply_reduce_fusion.2
  167.9 6.3 %psum.23 = f32[]{:T(128)} all-reduce(f32[]{:T(128)} %multiply_reduce_fusion.2), channel_id=1, replica_groups=mesh['groups'=2,'row'=4,'col'=4] {'row'}, use_global_device_ids=true, to_apply=%region_7.8 | all-reduce | flops 1 | bytes 8 | tf_op jit(solution)/shard_map/psum | solution.py:124
  174.2 10.7 %fusion = f32[512,1536]{1,0:T(8,128)S(1)} fusion(f32[768,768]{1,0:T(8,128)} %copy-done.24, f32[768,768]{1,0:T(8,128)} %copy-done.25, f32[512,128]{1,0:T(8,128)} %collective-permute-done.7, f32[128,512]{1,0:T(8,128)} %copy-done.29, f32[256,512]{1,0:T(8,128)} %copy-done.13, f32[128,512]{1,0:T(8,128)} %copy-done.28, f32[512,128]{1,0:T(8,128)} %collective-permute-done.6), kind=kOutput, calls=%fused_computation.1 | convolution fusion | flops 7250509824 | bytes 9437184 | tf_op jit(solution)/shard_map/dot_general | solution.py:35
  184.9 10.9 %fusion.25 = f32[1024,1536]{1,0:T(8,128)S(1)} fusion(f32[512,1536]{1,0:T(8,128)S(1)} %fusion, f32[512,512]{1,0:T(8,128)S(1)} %copy-done.6, f32[512,512]{1,0:T(8,128)S(1)} %copy-done.8), kind=kOutput, calls=%fused_computation.34 | convolution fusion | flops 9664200704 | bytes 11534336 | tf_op jit(solution)/shard_map/dot_general | solution.py:36
  195.9 0.8 multiply_add_fusion.1
  196.7 0.2 copy-done.10
  196.9 0.2 copy-done.12
  197.1 5.6 %fusion.7 = f32[512,1536]{1,0:T(8,128)S(1)} fusion(f32[512,768]{1,0:T(8,128)S(1)} %get-tuple-element.12, f32[512,768]{1,0:T(8,128)S(1)} %get-tuple-element.11, f32[256,512]{1,0:T(8,128)S(1)} %copy-done.12, f32[256,512]{1,0:T(8,128)S(1)} %copy-done.10), kind=kOutput, calls=%fused_computation.11 | convolution fusion | flops 4832886784 | bytes 7340032 | tf_op jit(solution)/shard_map/dot_general | solution.py:47
  202.7 1.4 slice_subtract_fusion.5
  204.7 5.6 %multiply_reduce_fusion = (f32[]{:T(128)}, f32[256,512]{1,0:T(8,128)}) fusion(f32[512,768]{1,0:T(8,128)S(1)} %get-tuple-element.29, f32[512,768]{1,0:T(8,128)S(1)} %copy-done.4, f32[256,768]{1,0:T(8,128)} %get-tuple-element.16, f32[256,768]{1,0:T(8,128)} %get-tuple-element.15), kind=kOutput, calls=%fused_computation.138 | convolution fusion | flops 2417491968 | bytes 5242884 | tf_op jit(solution)/shard_map/dot_general | solution.py:54
  210.3 33.3 %all-reduce = (f32[]{:T(128)}, f32[]{:T(128)}) all-reduce(f32[]{:T(128)} %get-tuple-element.37, f32[]{:T(128)} %get-tuple-element.39), channel_id=1, replica_groups=mesh['groups'=2,'row'=4,'col'=4] {'row','col'}, use_global_device_ids=true, to_apply=%region_1.2 | all-reduce | flops 2 | bytes 16 | tf_op jit(solution)/shard_map/psum | solution.py:97
  244.3 0.6 multiply_subtract_fusion.4
  246.2 2.1 multiply_subtract_fusion.3
  (60 shorter events, 0.3 us)
Async XLA Ops:
  7.2 145.6 %reduce-scatter.2.cloned.1.call-start = ((), (), s32[]{:S(2)}) async-start(), calls=%async_computation.1 | async-start | bytes 327680 | tf_op jit(solution)/shard_map/reduce_scatter | solution.py:121
  8.3 55.3 %collective-permute-start = (f32[128,512]{1,0:T(8,128)S(1)}, f32[128,512]{1,0:T(8,128)S(1)}, u32[]{:S(2)}, u32[]{:S(2)}) collective-permute-start(f32[128,512]{1,0:T(8,128)S(1)} %get-tuple-element.26), channel_id=1, source_target_pairs={{0,4},{4,8},{8,12},{1,5},{5,9},{9,13},{2,6},{6,10},{10,14},{3,7},{... | collective-permute-start | bytes 786440 | tf_op jit(solution)/shard_map/ppermute | solution.py:16
  10.7 53.0 %collective-permute-start.1 = (f32[128,512]{1,0:T(8,128)S(1)}, f32[128,512]{1,0:T(8,128)S(1)}, u32[]{:S(2)}, u32[]{:S(2)}) collective-permute-start(f32[128,512]{1,0:T(8,128)S(1)} %get-tuple-element.25), channel_id=1, source_target_pairs={{4,0},{8,4},{12,8},{5,1},{9,5},{13,9},{6,2},{10,6},{14,10},{7,3},{... | collective-permute-start | bytes 786440 | tf_op jit(solution)/shard_map/ppermute | solution.py:19
  12.0 6.4 %copy-start.27 = (f32[64,256]{1,0:T(8,128)S(1)}, f32[64,256]{1,0:T(8,128)}, u32[]{:S(2)}) copy-start(f32[64,256]{1,0:T(8,128)} %param.5) | copy-start | bytes 196612
  16.2 19.6 %copy-start.14 = (f32[256,768]{1,0:T(8,128)}, f32[256,768]{1,0:T(8,128)S(1)}, u32[]{:S(2)}) copy-start(f32[256,768]{1,0:T(8,128)S(1)} %get-tuple-element.32) | copy-start | bytes 2359300
  18.4 20.2 %copy-start.19 = (f32[256,512]{1,0:T(8,128)}, f32[256,512]{1,0:T(8,128)S(1)}, u32[]{:S(2)}) copy-start(f32[256,512]{1,0:T(8,128)S(1)} %get-tuple-element.35) | copy-start | bytes 1572868
  18.4 20.2 %copy-start.21 = (f32[256,512]{1,0:T(8,128)}, f32[256,512]{1,0:T(8,128)S(1)}, u32[]{:S(2)}) copy-start(f32[256,512]{1,0:T(8,128)S(1)} %get-tuple-element.36) | copy-start | bytes 1572868
  59.0 18.4 %copy-start.24 = (f32[768,768]{1,0:T(8,128)}, f32[768,768]{1,0:T(8,128)S(1)}, u32[]{:S(2)}) copy-start(f32[768,768]{1,0:T(8,128)S(1)} %get-tuple-element.41) | copy-start | bytes 7077892
  59.1 18.4 %copy-start.25 = (f32[768,768]{1,0:T(8,128)}, f32[768,768]{1,0:T(8,128)S(1)}, u32[]{:S(2)}) copy-start(f32[768,768]{1,0:T(8,128)S(1)} %get-tuple-element.42) | copy-start | bytes 7077892
  59.1 4.6 %copy-start.18 = (f32[256,512]{1,0:T(8,128)S(1)}, f32[256,512]{1,0:T(8,128)}, u32[]{:S(2)}) copy-start(f32[256,512]{1,0:T(8,128)} %param.4) | copy-start | bytes 1572868
  63.6 21.6 %copy-start.5 = (f32[512,512]{1,0:T(8,128)}, f32[512,512]{1,0:T(8,128)S(1)}, u32[]{:S(2)}) copy-start(f32[512,512]{1,0:T(8,128)S(1)} %get-tuple-element.43) | copy-start | bytes 3145732
  63.6 21.6 %copy-start.7 = (f32[512,512]{1,0:T(8,128)}, f32[512,512]{1,0:T(8,128)S(1)}, u32[]{:S(2)}) copy-start(f32[512,512]{1,0:T(8,128)S(1)} %get-tuple-element.44) | copy-start | bytes 3145732
  63.8 9.5 %collective-permute-start.2 = (f32[512,128]{1,0:T(8,128)S(1)}, f32[512,128]{1,0:T(8,128)S(1)}, u32[]{:S(2)}, u32[]{:S(2)}) collective-permute-start(f32[512,128]{1,0:T(8,128)S(1)} %get-tuple-element.21), channel_id=1, source_target_pairs={{0,1},{1,2},{2,3},{4,5},{5,6},{6,7},{8,9},{9,10},{10,11},{12,13},{... | collective-permute-start | bytes 786440 | tf_op jit(solution)/shard_map/ppermute | solution.py:16
  67.3 10.2 %collective-permute-start.3 = (f32[512,128]{1,0:T(8,128)S(1)}, f32[512,128]{1,0:T(8,128)S(1)}, u32[]{:S(2)}, u32[]{:S(2)}) collective-permute-start(f32[512,128]{1,0:T(8,128)S(1)} %get-tuple-element.22), channel_id=1, source_target_pairs={{1,0},{2,1},{3,2},{5,4},{6,5},{7,6},{9,8},{10,9},{11,10},{13,12},{... | collective-permute-start | bytes 786440 | tf_op jit(solution)/shard_map/ppermute | solution.py:19
  99.5 2.9 %copy-start.9 = (f32[256,512]{1,0:T(8,128)S(1)}, f32[256,512]{1,0:T(8,128)}, u32[]{:S(2)}) copy-start(f32[256,512]{1,0:T(8,128)} %get-tuple-element.33) | copy-start | bytes 1572868
  99.5 2.9 %copy-start.11 = (f32[256,512]{1,0:T(8,128)S(1)}, f32[256,512]{1,0:T(8,128)}, u32[]{:S(2)}) copy-start(f32[256,512]{1,0:T(8,128)} %get-tuple-element.34) | copy-start | bytes 1572868
  99.5 3.1 %copy-start.16 = (f32[512,768]{1,0:T(8,128)S(1)}, f32[512,768]{1,0:T(8,128)}, u32[]{:S(2)}) copy-start(f32[512,768]{1,0:T(8,128)} %get-tuple-element.4) | copy-start | bytes 4718596
  108.0 1.4 copy-start.3
  108.0 1.5 copy-start.26
  109.5 3.7 %copy-start.17 = (f32[512,768]{1,0:T(8,128)S(1)}, f32[512,768]{1,0:T(8,128)}, u32[]{:S(2)}) copy-start(f32[512,768]{1,0:T(8,128)} %get-tuple-element.27) | copy-start | bytes 4718596
  113.3 2.8 %copy-start.13 = (f32[256,512]{1,0:T(8,128)}, f32[256,512]{1,0:T(8,128)S(1)}, u32[]{:S(2)}) copy-start(f32[256,512]{1,0:T(8,128)S(1)} %get-tuple-element.38) | copy-start | bytes 1572868
  116.1 5.6 %copy-start.1 = (f32[512,768]{1,0:T(8,128)S(1)}, f32[512,768]{1,0:T(8,128)}, u32[]{:S(2)}) copy-start(f32[512,768]{1,0:T(8,128)} %get-tuple-element.5) | copy-start | bytes 4718596
  116.1 5.6 %copy-start.2 = (f32[512,768]{1,0:T(8,128)S(1)}, f32[512,768]{1,0:T(8,128)}, u32[]{:S(2)}) copy-start(f32[512,768]{1,0:T(8,128)} %get-tuple-element.6) | copy-start | bytes 4718596
  121.7 1.0 copy-start.20
  121.7 1.2 copy-start.22
  128.8 1.1 copy-start.15
  128.8 1.4 copy-start.23
  133.4 2.6 %collective-permute-start.4 = (f32[128,512]{1,0:T(8,128)S(1)}, f32[128,512]{1,0:T(8,128)S(1)}, u32[]{:S(2)}, u32[]{:S(2)}) collective-permute-start(f32[128,512]{1,0:T(8,128)S(1)} %get-tuple-element.23), channel_id=1, source_target_pairs={{0,4},{4,8},{8,12},{1,5},{5,9},{9,13},{2,6},{6,10},{10,14},{3,7},{... | collective-permute-start | bytes 786440 | tf_op jit(solution)/shard_map/ppermute | solution.py:16
  134.7 5.2 %collective-permute-start.5 = (f32[128,512]{1,0:T(8,128)S(1)}, f32[128,512]{1,0:T(8,128)S(1)}, u32[]{:S(2)}, u32[]{:S(2)}) collective-permute-start(f32[128,512]{1,0:T(8,128)S(1)} %get-tuple-element.24), channel_id=1, source_target_pairs={{4,0},{8,4},{12,8},{5,1},{9,5},{13,9},{6,2},{10,6},{14,10},{7,3},{... | collective-permute-start | bytes 786440 | tf_op jit(solution)/shard_map/ppermute | solution.py:19
  136.0 11.8 %copy-start.28 = (f32[128,512]{1,0:T(8,128)}, f32[128,512]{1,0:T(8,128)S(1)}, u32[]{:S(2)}) copy-start(f32[128,512]{1,0:T(8,128)S(1)} %collective-permute-done.4) | copy-start | bytes 786436
  139.9 0.7 copy-start.29
  142.4 31.8 %collective-permute-start.6 = (f32[512,128]{1,0:T(8,128)}, f32[512,128]{1,0:T(8,128)}, u32[]{:S(2)}, u32[]{:S(2)}) collective-permute-start(f32[512,128]{1,0:T(8,128)} %get-tuple-element.19), channel_id=1, source_target_pairs={{0,1},{1,2},{2,3},{4,5},{5,6},{6,7},{8,9},{9,10},{10,11},{12,13},{... | collective-permute-start | bytes 786440 | tf_op jit(solution)/shard_map/ppermute | solution.py:16
  146.5 27.7 %collective-permute-start.7 = (f32[512,128]{1,0:T(8,128)}, f32[512,128]{1,0:T(8,128)}, u32[]{:S(2)}, u32[]{:S(2)}) collective-permute-start(f32[512,128]{1,0:T(8,128)} %get-tuple-element.20), channel_id=1, source_target_pairs={{1,0},{2,1},{3,2},{5,4},{6,5},{7,6},{9,8},{10,9},{11,10},{13,12},{... | collective-permute-start | bytes 786440 | tf_op jit(solution)/shard_map/ppermute | solution.py:19
  174.2 10.7 %copy-start.6 = (f32[512,512]{1,0:T(8,128)S(1)}, f32[512,512]{1,0:T(8,128)}, u32[]{:S(2)}) copy-start(f32[512,512]{1,0:T(8,128)} %copy-done.5) | copy-start | bytes 3145732
  174.2 10.7 %copy-start.8 = (f32[512,512]{1,0:T(8,128)S(1)}, f32[512,512]{1,0:T(8,128)}, u32[]{:S(2)}) copy-start(f32[512,512]{1,0:T(8,128)} %copy-done.7) | copy-start | bytes 3145732
  184.9 10.9 %copy-start = (f32[512,768]{1,0:T(8,128)S(1)}, f32[512,768]{1,0:T(8,128)}, u32[]{:S(2)}) copy-start(f32[512,768]{1,0:T(8,128)} %get-tuple-element.8) | copy-start | bytes 4718596
  195.9 1.0 copy-start.10
  195.9 1.2 copy-start.12
  202.7 2.0 copy-start.4
Sparse Core Ops, SparseCore 0:
  132.4 20.2 reduce-scatter.1
